TPU v7x, 32 devices: a whole 2x2x4 slice. The times are simulated.
32 devices in a mesh: dp: 4 (over x, core), seq: 8 (over z, y).
Axes of the slice: x: 2, y: 2, z: 4, core: 2. Of those that a mesh axis runs over, the one named last changes fastest.
Arguments:
- tokens: bfloat16 [4, 4096, 1024], P('dp', 'seq'), may hold values from -6 to 6
- cotangent: bfloat16 [4, 4096, 1024], P('dp', 'seq'), may hold values from -6 to 6
- norm1_gain: float32 [1024], replicated, may hold values from 0.5 to 1.5
- norm1_bias: float32 [1024], replicated, may hold values from -1.25 to 1.25
- in_weight: bfloat16 [1024, 3072], replicated, may hold values from -0.1875 to 0.1875
- in_bias: float32 [3072], replicated, may hold values from -1.25 to 1.25
- short_weight: float32 [3, 3, 1024], P(None, None, 'seq'), may hold values from -3.5 to 3.5
- short_bias: float32 [3, 1024], P(None, 'seq'), may hold values from -1.25 to 1.25
- filter_in: float32 [33, 64], replicated, may hold values from -2 to 2
- filter_in_bias: float32 [64], replicated, may hold values from -3 to 3
- sine_freq: float32 [64], replicated, may hold values from 0.5 to 2
- filter_out: float32 [64, 1024], P(None, 'seq'), may hold values from -0.03125 to 0.03125
- decay_rates: float32 [1024], P('seq'), may hold values from 2 to 64
- filter_bias: float32 [1024], P('seq'), may hold values from -6 to 6
- out_weight: bfloat16 [1024, 1024], replicated, may hold values from -0.1875 to 0.1875
- out_bias: float32 [1024], replicated, may hold values from -1.25 to 1.25
- norm2_gain: float32 [1024], replicated, may hold values from 0.5 to 1.5
- norm2_bias: float32 [1024], replicated, may hold values from -1.25 to 1.25
- up_weight: bfloat16 [1024, 4096], replicated, may hold values from -0.1875 to 0.1875
- up_bias: float32 [4096], replicated, may hold values from -1.25 to 1.25
- down_weight: bfloat16 [4096, 1024], replicated, may hold values from -0.125 to 0.125
- down_bias: float32 [1024], replicated, may hold values from -1.25 to 1.25
Outputs:
- block_output: bfloat16 [4, 4096, 1024], P('dp', 'seq')
- grad_tokens: float32 [4, 4096, 1024], P('dp', 'seq')
- grad_norm1_gain: float32 [1024], replicated
- grad_norm1_bias: float32 [1024], replicated
- grad_in_weight: float32 [1024, 3072], P('seq', 'dp')
- grad_in_bias: float32 [3072], replicated
- grad_short_weight: float32 [3, 3, 1024], P(None, None, 'seq')
- grad_short_bias: float32 [3, 1024], P(None, 'seq')
- grad_filter_in: float32 [33, 64], replicated
- grad_filter_in_bias: float32 [64], replicated
- grad_sine_freq: float32 [64], replicated
- grad_filter_out: float32 [64, 1024], P(None, 'seq')
- grad_filter_bias: float32 [1024], P('seq')
- grad_out_weight: float32 [1024, 1024], P('seq', 'dp')
- grad_out_bias: float32 [1024], replicated
- grad_norm2_gain: float32 [1024], replicated
- grad_norm2_bias: float32 [1024], replicated
- grad_up_weight: float32 [1024, 4096], P('seq', 'dp')
- grad_up_bias: float32 [4096], replicated
- grad_down_weight: float32 [4096, 1024], P('seq', 'dp')
- grad_down_bias: float32 [1024], replicated
All inputs are finite; a program needn't handle non-finite values.
Results may differ from a plain program's by a relative error of at most 0.014.
Values may be sent and summed in bfloat16 or wider, within the bound.
No kernel may reach another device: no remote copies, remote signals or barrier semaphores. Data moves between devices by JAX's collectives and lax.ppermute only.
A program may use at most 320 MiB of HBM per device.

v0:
```python
import math
import jax
import jax.numpy as jnp
from jax import lax
from jax.sharding import PartitionSpec as P

EMB = 33
HIGH = lax.Precision.HIGHEST
EPSILON = 1e-05


def layer_norm(values, scale_vec, shift_vec):
    average = jnp.mean(values, axis=-1, keepdims=True)
    centred = values - average
    variance = jnp.mean(centred * centred, axis=-1, keepdims=True)
    return centred * lax.rsqrt(variance + EPSILON) * scale_vec + shift_vec


def position_features(length):
    steps = jnp.arange(length, dtype=jnp.float32)
    scaled = steps / (length - 1)
    angles = 2.0 * math.pi * steps / length
    bands = (EMB - 1) // 2
    freqs = 0.0001 + jnp.arange(bands, dtype=jnp.float32) * (bands - 1 - 0.0001) / (bands - 1)
    phase = freqs[:, None] * angles[None, :]
    return jnp.concatenate([scaled[None, :], jnp.cos(phase), -jnp.sin(phase)], axis=0)


def make_filter(filter_in, in_shift, sine_freq, filter_out, decay_rates, features):
    hidden_pre = jnp.dot(filter_in.T, features, precision=HIGH) + in_shift[:, None]
    hidden = jnp.sin(sine_freq[:, None] * hidden_pre)
    raw_kernel = jnp.dot(filter_out.T, hidden, precision=HIGH)
    return raw_kernel * jnp.exp(-decay_rates[:, None] * features[0][None, :])


def split_length(full_length):
    leading = 2
    while leading * leading * 2 <= full_length and full_length % (leading * 2) == 0:
        leading = leading * 2
    return (leading, full_length // leading)


def dft_tables(count_p, count_q):
    full_length = count_p * count_q
    index_p = jnp.arange(count_p, dtype=jnp.int32)
    index_q = jnp.arange(count_q, dtype=jnp.int32)
    prod_p = index_p[:, None] * index_p[None, :] % count_p
    prod_q = index_q[:, None] * index_q[None, :] % count_q
    prod_t = index_p[:, None] * index_q[None, :] % full_length
    angle_p = 2.0 * math.pi * prod_p.astype(jnp.float32) / count_p
    angle_q = 2.0 * math.pi * prod_q.astype(jnp.float32) / count_q
    angle_t = 2.0 * math.pi * prod_t.astype(jnp.float32) / full_length
    return (
        jnp.cos(angle_p),
        jnp.sin(angle_p),
        jnp.cos(angle_q),
        jnp.sin(angle_q),
        jnp.cos(angle_t),
        jnp.sin(angle_t),
    )


def forward_real(signal, tables):
    cos_p, sin_p, cos_q, sin_q, cos_t, sin_t = tables
    half_rows = cos_p.shape[0] // 2
    count_q = cos_q.shape[0]
    blocked = signal.reshape(signal.shape[0], half_rows, count_q)
    part_re = jnp.einsum("kn,cnq->ckq", cos_p[:, :half_rows], blocked, precision=HIGH)
    part_im = -jnp.einsum("kn,cnq->ckq", sin_p[:, :half_rows], blocked, precision=HIGH)
    turned_re = part_re * cos_t + part_im * sin_t
    turned_im = part_im * cos_t - part_re * sin_t
    spec_re = jnp.einsum("ckn,nm->ckm", turned_re, cos_q, precision=HIGH) + jnp.einsum(
        "ckn,nm->ckm", turned_im, sin_q, precision=HIGH
    )
    spec_im = jnp.einsum("ckn,nm->ckm", turned_im, cos_q, precision=HIGH) - jnp.einsum(
        "ckn,nm->ckm", turned_re, sin_q, precision=HIGH
    )
    return (spec_re, spec_im)


def inverse_real(spec_re, spec_im, tables):
    cos_p, sin_p, cos_q, sin_q, cos_t, sin_t = tables
    half_rows = cos_p.shape[0] // 2
    full_length = cos_p.shape[0] * cos_q.shape[0]
    back_re = jnp.einsum("ckm,nm->ckn", spec_re, cos_q, precision=HIGH) - jnp.einsum(
        "ckm,nm->ckn", spec_im, sin_q, precision=HIGH
    )
    back_im = jnp.einsum("ckm,nm->ckn", spec_im, cos_q, precision=HIGH) + jnp.einsum(
        "ckm,nm->ckn", spec_re, sin_q, precision=HIGH
    )
    twist_re = back_re * cos_t - back_im * sin_t
    twist_im = back_im * cos_t + back_re * sin_t
    result = jnp.einsum("nk,ckq->cnq", cos_p[:half_rows], twist_re, precision=HIGH) - jnp.einsum(
        "nk,ckq->cnq", sin_p[:half_rows], twist_im, precision=HIGH
    )
    return result.reshape(spec_re.shape[0], full_length // 2) / full_length


def mixer(
    received,
    short_taps,
    tap_shift,
    filter_in,
    in_shift,
    sine_freq,
    filter_out,
    filter_shift,
    decay_rates,
    features,
    tables,
):
    length = received.shape[2]
    shifted_one = jnp.pad(received, ((0, 0), (0, 0), (1, 0)))[:, :, :length]
    shifted_two = jnp.pad(received, ((0, 0), (0, 0), (2, 0)))[:, :, :length]
    short = (
        tap_shift[:, :, None]
        + short_taps[0][:, :, None] * shifted_two
        + short_taps[1][:, :, None] * shifted_one
        + short_taps[2][:, :, None] * received
    )
    gate_out, gate_in, values = (short[0], short[1], short[2])
    kernel = make_filter(filter_in, in_shift, sine_freq, filter_out, decay_rates, features)
    inner = values * gate_in
    inner_re, inner_im = forward_real(inner, tables)
    kernel_re, kernel_im = forward_real(kernel, tables)
    conv = inverse_real(
        inner_re * kernel_re - inner_im * kernel_im,
        inner_re * kernel_im + inner_im * kernel_re,
        tables,
    )
    conv = conv + inner * filter_shift[:, None]
    return conv * gate_out


def reduce_matrices(matrix_grads):
    partial_sums = (
        lax.psum_scatter(matrix_grads[0], "seq", scatter_dimension=0, tiled=True),
        lax.psum_scatter(matrix_grads[1], "seq", scatter_dimension=0, tiled=True),
        lax.psum_scatter(matrix_grads[2], "seq", scatter_dimension=0, tiled=True),
        lax.psum_scatter(matrix_grads[3], "seq", scatter_dimension=0, tiled=True),
    )
    reduced = (
        lax.psum_scatter(partial_sums[0], "dp", scatter_dimension=1, tiled=True),
        lax.psum_scatter(partial_sums[1], "dp", scatter_dimension=1, tiled=True),
        lax.psum_scatter(partial_sums[2], "dp", scatter_dimension=1, tiled=True),
        lax.psum_scatter(partial_sums[3], "dp", scatter_dimension=1, tiled=True),
    )
    return reduced


def on_device(
    tokens,
    cotangent,
    norm1_gain,
    norm1_bias,
    in_weight,
    in_bias,
    short_weight,
    short_bias,
    filter_in,
    filter_in_bias,
    sine_freq,
    filter_out,
    decay_rates,
    filter_bias,
    out_weight,
    out_bias,
    norm2_gain,
    norm2_bias,
    up_weight,
    up_bias,
    down_weight,
    down_bias,
):
    model_width = in_weight.shape[0]
    tok_rows = tokens.shape[1]
    group_size = lax.axis_size("seq")
    length = tok_rows * group_size
    local_tokens = tokens[0].astype(jnp.float32)
    normed, norm1_pull = jax.vjp(layer_norm, local_tokens, norm1_gain, norm1_bias)
    normed_low = normed.astype(jnp.bfloat16)
    in_three = in_weight.reshape(model_width, 3, model_width)
    projected = jnp.einsum("td,dkc->kct", normed_low, in_three, preferred_element_type=jnp.float32)
    projected = projected + in_bias.reshape(3, model_width)[:, :, None]
    received = lax.all_to_all(
        projected.astype(jnp.bfloat16), "seq", split_axis=1, concat_axis=2, tiled=True
    )
    features = position_features(length)
    count_p, count_q = split_length(2 * length)
    tables = dft_tables(count_p, count_q)

    def local_mixer(
        recv_values, taps, tap_shift, first_layer, first_shift, freqs, last_layer, direct_shift
    ):
        return mixer(
            recv_values,
            taps,
            tap_shift,
            first_layer,
            first_shift,
            freqs,
            last_layer,
            direct_shift,
            decay_rates,
            features,
            tables,
        )

    mixed, mixer_pull = jax.vjp(
        local_mixer,
        received.astype(jnp.float32),
        short_weight,
        short_bias,
        filter_in,
        filter_in_bias,
        sine_freq,
        filter_out,
        filter_bias,
    )
    returned = lax.all_to_all(
        mixed.astype(jnp.bfloat16), "seq", split_axis=1, concat_axis=0, tiled=True
    )
    attended = (
        jnp.einsum("ct,ce->te", returned, out_weight, preferred_element_type=jnp.float32) + out_bias
    )
    resid = local_tokens + attended
    normed2, norm2_pull = jax.vjp(layer_norm, resid, norm2_gain, norm2_bias)
    normed2_low = normed2.astype(jnp.bfloat16)
    up_pre = jnp.dot(normed2_low, up_weight, preferred_element_type=jnp.float32) + up_bias
    activated, gelu_pull = jax.vjp(jax.nn.gelu, up_pre)
    activated_low = activated.astype(jnp.bfloat16)
    block_out = (
        resid + jnp.dot(activated_low, down_weight, preferred_element_type=jnp.float32) + down_bias
    )
    grad_out = cotangent[0]
    grad_down = jnp.einsum("tf,td->fd", activated_low, grad_out, preferred_element_type=jnp.float32)
    grad_down_bias = jnp.sum(grad_out.astype(jnp.float32), axis=0)
    grad_activated = jnp.einsum(
        "td,fd->tf", grad_out, down_weight, preferred_element_type=jnp.float32
    )
    grad_up_pre = gelu_pull(grad_activated)[0].astype(jnp.bfloat16)
    grad_up = jnp.einsum("td,tf->df", normed2_low, grad_up_pre, preferred_element_type=jnp.float32)
    grad_up_bias = jnp.sum(grad_up_pre.astype(jnp.float32), axis=0)
    grad_normed2 = jnp.einsum(
        "tf,df->td", grad_up_pre, up_weight, preferred_element_type=jnp.float32
    )
    grad_resid_norm, grad_gain2, grad_shift2 = norm2_pull(grad_normed2)
    grad_resid = grad_out.astype(jnp.float32) + grad_resid_norm
    grad_attn = grad_resid.astype(jnp.bfloat16)
    grad_out_weight = jnp.einsum(
        "ct,te->ce", returned, grad_attn, preferred_element_type=jnp.float32
    )
    grad_out_bias = jnp.sum(grad_attn.astype(jnp.float32), axis=0)
    grad_mixed_rows = jnp.einsum(
        "te,ce->ct", grad_attn, out_weight, preferred_element_type=jnp.float32
    )
    grad_mixed = lax.all_to_all(
        grad_mixed_rows.astype(jnp.bfloat16), "seq", split_axis=0, concat_axis=1, tiled=True
    )
    (
        grad_received,
        grad_taps,
        grad_tap_shift,
        grad_first,
        grad_first_shift,
        grad_freqs,
        grad_last,
        grad_direct,
    ) = mixer_pull(grad_mixed.astype(jnp.float32))
    grad_proj = lax.all_to_all(
        grad_received.astype(jnp.bfloat16), "seq", split_axis=2, concat_axis=1, tiled=True
    )
    grad_in = jnp.einsum("td,kct->dkc", normed_low, grad_proj, preferred_element_type=jnp.float32)
    grad_in = grad_in.reshape(model_width, 3 * model_width)
    grad_in_bias = jnp.sum(grad_proj.astype(jnp.float32), axis=2).reshape(3 * model_width)
    grad_normed = jnp.einsum("kct,dkc->td", grad_proj, in_three, preferred_element_type=jnp.float32)
    grad_tokens_norm, grad_gain1, grad_shift1 = norm1_pull(grad_normed)
    grad_tokens = grad_resid + grad_tokens_norm
    matrix_sums = reduce_matrices((grad_in, grad_out_weight, grad_up, grad_down))
    shared = lax.psum(
        (
            grad_gain1,
            grad_shift1,
            grad_in_bias,
            grad_out_bias,
            grad_gain2,
            grad_shift2,
            grad_up_bias,
            grad_down_bias,
            grad_first,
            grad_first_shift,
            grad_freqs,
        ),
        ("dp", "seq"),
    )
    channel = lax.psum((grad_taps, grad_tap_shift, grad_last, grad_direct), "dp")
    return (
        block_out.astype(jnp.bfloat16)[None],
        grad_tokens[None],
        shared[0],
        shared[1],
        matrix_sums[0],
        shared[2],
        channel[0],
        channel[1],
        shared[8],
        shared[9],
        shared[10],
        channel[2],
        channel[3],
        matrix_sums[1],
        shared[3],
        shared[4],
        shared[5],
        matrix_sums[2],
        shared[6],
        matrix_sums[3],
        shared[7],
    )


def solution(mesh):
    in_specs = (
        P("dp", "seq", None),
        P("dp", "seq", None),
        P(),
        P(),
        P(),
        P(),
        P(None, None, "seq"),
        P(None, "seq"),
        P(),
        P(),
        P(),
        P(None, "seq"),
        P("seq"),
        P("seq"),
        P(),
        P(),
        P(),
        P(),
        P(),
        P(),
        P(),
        P(),
    )
    out_specs = (
        P("dp", "seq", None),
        P("dp", "seq", None),
        P(),
        P(),
        P("seq", "dp"),
        P(),
        P(None, None, "seq"),
        P(None, "seq"),
        P(),
        P(),
        P(),
        P(None, "seq"),
        P("seq"),
        P("seq", "dp"),
        P(),
        P(),
        P(),
        P("seq", "dp"),
        P(),
        P("seq", "dp"),
        P(),
    )
    return jax.shard_map(
        on_device, mesh=mesh, in_specs=in_specs, out_specs=out_specs, check_vma=False
    )
```

profile of v0, /device:TPU:0, one launch (start us, length us, event | category | flops | bytes accessed | tf_op | source)
XLA Modules:
  0.0 1629.9 jit_solution(7584546690204504811)
XLA Ops:
  56.7 9.5 fusion.128
  66.2 70.4 %all-to-all-done = bf16[3,1024,512]{2,0,1:T(4,128)(2,1)} async-done(((bf16[3,1024,512]{2,0,1:T(4,128)(2,1)}), bf16[3,1024,512]{2,0,1:T(4,128)(2,1)}, u32[]{:S(2)}, u32[]{:S(2)}) %all-to-all-start) | async-done | bytes 3145760 | tf_op jit(solution)/shard_map/all_to_all | solution.py:185
  160.5 9.3 fusion.132
  169.9 9.6 fusion.134
  179.4 12.3 fusion.24
  211.7 9.2 fusion.64
  220.9 9.6 fusion.88
  230.5 9.1 fusion.91
  239.6 9.4 fusion.82
  249.0 14.2 multiply_subtract_fusion
  280.8 18.1 %fusion.44 = f32[128,64,64]{0,2,1:T(8,128)S(1)} fusion(f32[128,64]{0,1:T(8,128)S(1)} %get-tuple-element.104, f32[128,64]{0,1:T(8,128)S(1)} %get-tuple-element.105, f32[128,128,64]{1,2,0:T(8,128)S(1)} %fusion.185, f32[128,128,64]{1,2,0:T(8,128)S(1)} %fusion.203, f32[128,128,64]{1,2,0:T(8,128)S(1)} %fusion.183, f32[128,128,64]{1,2,0:T(8,128)S(1)} %fusion.201, ...), kind=kOutput, calls=%fused_computation.89 | convolution fusion | flops 810549248 | bytes 19005440 | tf_op jit(solution)/shard_map/jvp(nk,ckq->cnq)/dot_general | solution.py:93
  298.9 21.2 %multiply_bitcast_fusion = f32[128,64,64]{0,1,2:T(8,128)S(1)} fusion(f32[128,64,64]{0,2,1:T(8,128)S(1)} %fusion.44, f32[128,64]{0,1:T(8,128)S(1)} %get-tuple-element.104, f32[128,64]{0,1:T(8,128)S(1)} %get-tuple-element.105, f32[128,128,64]{1,2,0:T(8,128)S(1)} %fusion.185, f32[128,128,64]{1,2,0:T(8,128)S(1)} %fusion.203, f32[128,128,64]{1,2,0:T(8,128)S(1)} %fusion.183, ...), kind=kOutput, calls=%fused_computation.185 | convolution fusion | flops 811597824 | bytes 21102592 | tf_op jit(solution)/shard_map/jvp(nk,ckq->cnq)/dot_general | solution.py:93
  322.0 29.5 %all_to_all.56 = bf16[128,8,512]{0,2,1:T(8,128)(2,1)} all-to-all(bf16[128,8,512]{0,2,1:T(8,128)(2,1)S(1)} %fusion.119), channel_id=1, replica_groups=mesh['dp'=4,'seq'=8] {'seq'}, dimensions={1} | all-to-all | bytes 2097152 | tf_op jit(solution)/shard_map/all_to_all | solution.py:220
  356.8 10.8 fusion.354
  367.6 16.2 convert_reduce_fusion
  405.5 36.1 %all-to-all-done.2 = bf16[8,128,512]{1,2,0:T(8,128)(2,1)} async-done(((bf16[8,128,512]{1,2,0:T(8,128)(2,1)}), bf16[8,128,512]{1,2,0:T(8,128)(2,1)}, u32[]{:S(2)}, u32[]{:S(2)}) %all-to-all-start.2) | async-done | bytes 1048608 | tf_op jit(solution)/shard_map/all_to_all | solution.py:257
  466.6 9.6 fusion.38
  476.2 9.3 fusion.97
  485.5 17.6 %multiply_add_fusion.2 = (f32[128,128,64]{1,2,0:T(8,128)S(1)}, f32[128,128,64]{1,2,0:T(8,128)}, f32[128,128,64]{1,2,0:T(8,128)}, f32[128,128,64]{1,2,0:T(8,128)}) fusion(f32[128,128,64]{1,2,0:T(8,128)} %get-tuple-element.96, f32[128,128,64]{1,2,0:T(8,128)} %fusion.82, f32[128,128,64]{1,2,0:T(8,128)} %fusion.97, f32[128,128,64]{1,2,0:T(8,128)} %fusion.88, ...), kind=kOutput, calls=%fused_computation.84 | convolution fusion | flops 820043776 | bytes 46137344 | tf_op jit(solution)/shard_map/transpose(jvp(ckm,nm->ckn))/dot_general | solution.py:88
  538.8 12.2 fusion.14
  551.0 9.3 fusion.32
  589.9 20.0 %copy.246 = bf16[3,128,4096]{1,0,2:T(4,128)(2,1)S(1)} copy(bf16[3,128,4096]{1,2,0:T(8,128)(2,1)S(1)} %fusion.9) | data formatting | bytes 6291456 | tf_op jit(solution)/shard_map/convert_element_type | solution.py:271
  609.9 93.2 %all_to_all.57 = bf16[3,128,4096]{1,0,2:T(4,128)(2,1)S(1)} all-to-all(bf16[3,128,4096]{1,0,2:T(4,128)(2,1)S(1)} %copy.246), channel_id=1, replica_groups=mesh['dp'=4,'seq'=8] {'seq'}, dimensions={2} | all-to-all | bytes 6291456 | tf_op jit(solution)/shard_map/all_to_all | solution.py:270
  719.1 13.3 fusion.353
  732.5 15.8 fusion.145
  748.9 176.9 %reduce-scatter.9.cloned.1.call-done = f32[128,3072]{1,0:T(8,128)} async-done(((f32[1024,3072]{1,0:T(8,128)}), f32[128,3072]{1,0:T(8,128)}) %reduce-scatter.9.cloned.1.call-update) | async-done | bytes 1572880 | tf_op jit(solution)/shard_map/reduce_scatter | solution.py:137
  925.9 286.0 %reduce-scatter.17.cloned.1.call-done = f32[128,4096]{1,0:T(8,128)} async-done(((f32[1024,4096]{1,0:T(8,128)}), f32[128,4096]{1,0:T(8,128)}) %reduce-scatter.17.cloned.1.call-update) | async-done | bytes 2097168 | tf_op jit(solution)/shard_map/reduce_scatter | solution.py:139
  1212.2 13.0 fusion.143
  1242.0 255.4 %reduce-scatter.21.cloned.1.call-done = f32[512,1024]{1,0:T(8,128)} async-done(((f32[4096,1024]{1,0:T(8,128)}), f32[512,1024]{1,0:T(8,128)}) %reduce-scatter.21.cloned.1.call-update) | async-done | bytes 2097168 | tf_op jit(solution)/shard_map/reduce_scatter | solution.py:140
  1510.1 12.6 all-reduce.11
  1541.1 41.1 %all-reduce.10 = (f32[1024]{0:T(1024)}, f32[1024]{0:T(1024)}, f32[3072]{0:T(1024)}, f32[33,64]{1,0:T(8,128)}, f32[64]{0:T(128)}, /*index=5*/f32[64]{0:T(128)}, f...) all-reduce(f32[1024]{0:T(1024)S(1)} %get-tuple-element.29, ...), channel_id=1, replica_groups=mesh['dp'=4,'seq'=8] {'dp','seq'}, use_global_device_ids=true, to_apply=%region_9.10 | all-reduce | flops 15552 | bytes 124416 | tf_op jit(solution)/shard_map/psum | solution.py:280
  1588.3 34.5 %reduce-scatter.23.cloned.1.call-done = f32[512,256]{1,0:T(8,128)} async-done(((f32[512,1024]{1,0:T(8,128)}), f32[512,256]{1,0:T(8,128)}) %reduce-scatter.23.cloned.1.call-update) | async-done | bytes 524304 | tf_op jit(solution)/shard_map/reduce_scatter | solution.py:146
  (276 shorter events, 300.0 us)
Async XLA Ops:
  7.2 346.6 %copy-start = (bf16[1024,1024]{1,0:T(8,128)(2,1)S(1)}, bf16[1024,1024]{1,0:T(8,128)(2,1)}, u32[]{:S(2)}) copy-start(bf16[1024,1024]{1,0:T(8,128)(2,1)} %param.36) | copy-start | bytes 6291460
  35.4 101.2 %all-to-all-start = ((bf16[3,1024,512]{2,0,1:T(4,128)(2,1)}), bf16[3,1024,512]{2,0,1:T(4,128)(2,1)}, u32[]{:S(2)}, u32[]{:S(2)}) async-start(bf16[3,1024,512]{2,0,1:T(4,128)(2,1)} %copy.198), calls=%async_computation | async-start | bytes 8388608 | tf_op jit(solution)/shard_map/all_to_all | solution.py:185
  44.2 105.5 %copy-start.50 = (f32[3,128]{1,0:T(4,128)}, f32[3,128]{1,0:T(4,128)S(1)}, u32[]{:S(2)}) copy-start(f32[3,128]{1,0:T(4,128)S(1)} %get-tuple-element.94) | copy-start | bytes 4612
  44.3 105.5 %copy-start.52 = (f32[3,128]{1,0:T(4,128)}, f32[3,128]{1,0:T(4,128)S(1)}, u32[]{:S(2)}) copy-start(f32[3,128]{1,0:T(4,128)S(1)} %get-tuple-element.93) | copy-start | bytes 4612
  44.3 105.5 %copy-start.54 = (f32[3,128]{1,0:T(4,128)}, f32[3,128]{1,0:T(4,128)S(1)}, u32[]{:S(2)}) copy-start(f32[3,128]{1,0:T(4,128)S(1)} %get-tuple-element.95) | copy-start | bytes 4612
  160.5 160.8 %copy-start.2 = (f32[1,128,4096]{1,2,0:T(8,128)}, f32[1,128,4096]{1,2,0:T(8,128)S(1)}, u32[]{:S(2)}) copy-start(f32[1,128,4096]{1,2,0:T(8,128)S(1)} %get-tuple-element.80) | copy-start | bytes 6291460
  321.3 30.1 %copy-start.17 = (f32[128,64,64]{0,2,1:T(8,128)}, f32[128,64,64]{0,2,1:T(8,128)S(1)}, u32[]{:S(2)}) copy-start(f32[128,64,64]{0,2,1:T(8,128)S(1)} %copy.227) | copy-start | bytes 6291460
  321.7 32.1 %copy-start.40 = (f32[1024]{0:T(1024)S(1)}, f32[1024]{0:T(1024)}, u32[]{:S(2)}) copy-start(f32[1024]{0:T(1024)} %param.37) | copy-start | bytes 12292
  356.4 35.5 %copy-start.14 = (f32[512,1024]{1,0:T(8,128)}, f32[512,1024]{1,0:T(8,128)S(1)}, u32[]{:S(2)}) copy-start(f32[512,1024]{1,0:T(8,128)S(1)} %get-tuple-element.98) | copy-start | bytes 6291460
  356.8 27.0 %slice-start.4 = ((s8[8388608]{0:T(1024)(128)(4,1)}), s8[4194304]{0:T(1024)(128)(4,1)S(1)}, s32[]{:S(2)}) async-start(s8[8388608]{0:T(1024)(128)(4,1)} %bitcast.400), calls=%async_computation.24 | async-start | bytes 8388608
  367.6 16.2 slice-start.5
  396.4 45.3 %all-to-all-start.2 = ((bf16[8,128,512]{1,2,0:T(8,128)(2,1)}), bf16[8,128,512]{1,2,0:T(8,128)(2,1)}, u32[]{:S(2)}, u32[]{:S(2)}) async-start(bf16[8,128,512]{1,2,0:T(8,128)(2,1)} %bitcast.369), calls=%async_computation.2 | async-start | bytes 2097152 | tf_op jit(solution)/shard_map/all_to_all | solution.py:257
  400.6 347.7 %reduce-scatter.13.cloned.1.call-start = ((), (), s32[]{:S(2)}) async-start(), calls=%async_computation.14 | async-start | bytes 4718592 | tf_op jit(solution)/shard_map/reduce_scatter | solution.py:138
  405.3 37.7 %copy-start.16 = (f32[1,128,4096]{1,2,0:T(8,128)S(1)}, f32[1,128,4096]{1,2,0:T(8,128)}, u32[]{:S(2)}) copy-start(f32[1,128,4096]{1,2,0:T(8,128)} %get-tuple-element.81) | copy-start | bytes 6291460
  405.3 520.5 %reduce-scatter.9.cloned.1.call-start = ((), (), s32[]{:S(2)}) async-start(), calls=%async_computation.12 | async-start | bytes 14155776 | tf_op jit(solution)/shard_map/reduce_scatter | solution.py:137
  459.9 16.3 %copy-start.8 = (f32[128,128,64]{1,0,2:T(8,128)}, f32[128,128,64]{1,0,2:T(8,128)S(1)}, u32[]{:S(2)}) copy-start(f32[128,128,64]{1,0,2:T(8,128)S(1)} %get-tuple-element.71) | copy-start | bytes 12582916
  551.0 18.9 %slice-start.2 = ((s8[6291456]{0:T(1024)(128)(4,1)}), s8[4194304]{0:T(1024)(128)(4,1)S(1)}, s32[]{:S(2)}) async-start(s8[6291456]{0:T(1024)(128)(4,1)} %bitcast.378), calls=%async_computation.22 | async-start | bytes 8388608
  719.1 492.8 %reduce-scatter.17.cloned.1.call-start = ((), (), s32[]{:S(2)}) async-start(), calls=%async_computation.16 | async-start | bytes 18874368 | tf_op jit(solution)/shard_map/reduce_scatter | solution.py:139
  732.5 764.9 %reduce-scatter.21.cloned.1.call-start = ((), (), s32[]{:S(2)}) async-start(), calls=%async_computation.18 | async-start | bytes 18874368 | tf_op jit(solution)/shard_map/reduce_scatter | solution.py:140
  748.3 463.8 %copy-start.76 = (f32[1024]{0:T(1024)S(1)}, f32[1024]{0:T(1024)}, u32[]{:S(2)}) copy-start(f32[1024]{0:T(1024)} %param.43) | copy-start | bytes 12292
  748.3 833.9 %reduce-scatter.15.cloned.1.call-start = ((), (), s32[]{:S(2)}) async-start(), calls=%async_computation.15 | async-start | bytes 655360 | tf_op jit(solution)/shard_map/reduce_scatter | solution.py:144
  748.9 833.3 %reduce-scatter.11.cloned.1.call-start = ((), (), s32[]{:S(2)}) async-start(), calls=%async_computation.13 | async-start | bytes 1966080 | tf_op jit(solution)/shard_map/reduce_scatter | solution.py:143
  925.9 662.5 %reduce-scatter.19.cloned.1.call-start = ((), (), s32[]{:S(2)}) async-start(), calls=%async_computation.17 | async-start | bytes 2621440 | tf_op jit(solution)/shard_map/reduce_scatter | solution.py:145
  1211.9 410.9 %reduce-scatter.23.cloned.1.call-start = ((), (), s32[]{:S(2)}) async-start(), calls=%async_computation.19 | async-start | bytes 2621440 | tf_op jit(solution)/shard_map/reduce_scatter | solution.py:146
  1239.4 258.0 %copy-start.37 = (f32[4096]{0:T(1024)S(1)}, f32[4096]{0:T(1024)}, u32[]{:S(2)}) copy-start(f32[4096]{0:T(1024)} %copy-done.36) | copy-start | bytes 49156
  1239.4 258.0 %copy-start.68 = (f32[128]{0:T(128)S(1)}, f32[128]{0:T(128)}, u32[]{:S(2)}) copy-start(f32[128]{0:T(128)} %copy-done.67) | copy-start | bytes 1540
  1241.9 258.8 %copy-start.62 = (f32[64]{0:T(128)S(1)}, f32[64]{0:T(128)}, u32[]{:S(2)}) copy-start(f32[64]{0:T(128)} %param.32) | copy-start | bytes 772
  1500.8 21.9 %copy-start.39 = (f32[64,128]{1,0:T(8,128)S(1)}, f32[64,128]{1,0:T(8,128)}, u32[]{:S(2)}) copy-start(f32[64,128]{1,0:T(8,128)} %param.33) | copy-start | bytes 98308
  1507.5 22.6 %copy-start.30 = (f32[16,4096]{1,0:T(8,128)S(1)}, f32[16,4096]{1,0:T(8,128)}, u32[]{:S(2)}) copy-start(f32[16,4096]{1,0:T(8,128)} %copy-done.29) | copy-start | bytes 786436
  1507.5 22.6 %copy-start.35 = (f32[1,4096]{1,0:T(1,128)S(1)}, f32[1,4096]{1,0:T(1,128)}, u32[]{:S(2)}) copy-start(f32[1,4096]{1,0:T(1,128)} %copy-done.34) | copy-start | bytes 49156
  1510.1 20.0 %copy-start.32 = (f32[16,4096]{1,0:T(8,128)S(1)}, f32[16,4096]{1,0:T(8,128)}, u32[]{:S(2)}) copy-start(f32[16,4096]{1,0:T(8,128)} %copy-done.31) | copy-start | bytes 786436
  1538.3 84.5 %copy-start.1 = (bf16[1024,1024]{1,0:T(8,128)(2,1)S(1)}, bf16[1024,1024]{1,0:T(8,128)(2,1)}, u32[]{:S(2)}) copy-start(bf16[1024,1024]{1,0:T(8,128)(2,1)} %param.36) | copy-start | bytes 6291460
  (62 other events, 348.5 us)
Sparse Core Ops, SparseCore 0:
  405.4 97.9 reduce-scatter.12
  719.2 206.5 reduce-scatter.8
  930.1 281.7 reduce-scatter.16
  1215.5 281.7 reduce-scatter.20
  1500.4 21.0 reduce-scatter.14
  1524.4 28.4 reduce-scatter.10
  1556.2 32.0 reduce-scatter.18
  1591.4 31.3 reduce-scatter.22
where the time goes:
time: 1630 us
  waiting for transfers between devices  866 us (53%)
  matrix products  437 us (27%)
  blocking collectives  176 us (11%)
  local copies, waits for them, and re-layouts  68.8 us (4%)
  other arithmetic  52.5 us (3%)
    reduce_scatter x1, waiting for transfers between devices, reduce_matrices(): lax.psum_scatter(matrix_grads[2], 'seq', scatter_dimension=0, tiled=True)  286 us
    reduce_scatter x1, waiting for transfers between devices, reduce_matrices(): lax.psum_scatter(matrix_grads[3], 'seq', scatter_dimension=0, tiled=True)  255 us
    reduce_scatter x1, waiting for transfers between devices, reduce_matrices(): lax.psum_scatter(matrix_grads[0], 'seq', scatter_dimension=0, tiled=True)  177 us
    all_to_all x1, blocking collectives, on_device(): lax.all_to_all(grad_received.astype(jnp.bfloat16), 'seq', split_axis=2, c...  93.2 us
    all_to_all x1, waiting for transfers between devices, on_device(): lax.all_to_all(projected.astype(jnp.bfloat16), 'seq', split_axis=1, conca...  70.4 us
    dot_general x4, matrix products, forward_real(): jnp.einsum('ckn,nm->ckm', turned_re, sin_q, precision=HIGH)  41.6 us
    psum x1, blocking collectives, on_device(): lax.psum((grad_gain1, grad_shift1, grad_in_bias, grad_out_bias, grad_gain...  41.1 us
    dot_general x4, matrix products, forward_real(): jnp.einsum('kn,cnq->ckq', cos_p[:, :half_rows], blocked, precision=HIGH)  38.2 us
  transfers between devices with their start and end apart: 10, of which 7 were waited for; matrix products, arithmetic and copies ran while one was open for 18% of the time, Pallas kernels for 0%

commit v1 on v0

--- a/solution.py
+++ b/solution.py
@@ -182,9 +182,19 @@
     in_three = in_weight.reshape(model_width, 3, model_width)
     projected = jnp.einsum("td,dkc->kct", normed_low, in_three, preferred_element_type=jnp.float32)
     projected = projected + in_bias.reshape(3, model_width)[:, :, None]
-    received = lax.all_to_all(
-        projected.astype(jnp.bfloat16), "seq", split_axis=1, concat_axis=2, tiled=True
-    )
+    x = projected.astype(jnp.bfloat16)
+    ways, here = (lax.axis_size("seq"), lax.axis_index("seq"))
+    width = x.shape[1] // ways
+    shape = list(x.shape)
+    shape[1] = width
+    height = shape[2]
+    shape[2] = height * ways
+    received = jnp.zeros(shape, x.dtype)
+    for mask in range(ways):
+        part = lax.dynamic_slice_in_dim(x, (here ^ mask) * width, width, axis=1)
+        if mask:
+            part = lax.ppermute(part, "seq", [(d, d ^ mask) for d in range(ways)])
+        received = lax.dynamic_update_slice_in_dim(received, part, (here ^ mask) * height, axis=2)
     features = position_features(length)
     count_p, count_q = split_length(2 * length)
     tables = dft_tables(count_p, count_q)

time: 1630 us -> 1580 us (0.969)
  waiting for transfers between devices: 866 us -> 809 us
    all_to_all x1 -> x0, waiting for transfers between devices: 70.4 us -> none  [on_device(): lax.all_to_all(projected.astype(jnp.bfloat16), 'seq', split_axis=1, conca...]
  transfers between devices with their start and end apart: 10 -> 16, of which waited for: 7 -> 7; matrix products, arithmetic and copies ran while one was open for 18% -> 19% of each run, Pallas kernels for 0% -> 0%
where the time goes in v1:
time: 1580 us
  waiting for transfers between devices  809 us (51%)
  matrix products  437 us (28%)
  blocking collectives  188 us (12%)
  local copies, waits for them, and re-layouts  68.5 us (4%)
  other arithmetic  45.2 us (3%)
  starting transfers between devices  17.4 us (1%)
  between operations  15.8 us (1%)
    reduce_scatter x1, waiting for transfers between devices, reduce_matrices(): lax.psum_scatter(matrix_grads[2], 'seq', scatter_dimension=0, tiled=True)  286 us
    reduce_scatter x1, waiting for transfers between devices, reduce_matrices(): lax.psum_scatter(matrix_grads[3], 'seq', scatter_dimension=0, tiled=True)  255 us
    reduce_scatter x1, waiting for transfers between devices, reduce_matrices(): lax.psum_scatter(matrix_grads[0], 'seq', scatter_dimension=0, tiled=True)  177 us
    all_to_all x1, blocking collectives, on_device(): lax.all_to_all(grad_received.astype(jnp.bfloat16), 'seq', split_axis=2, c...  93.1 us
    dot_general x4, matrix products, forward_real(): jnp.einsum('ckn,nm->ckm', turned_re, sin_q, precision=HIGH)  41.6 us
    psum x1, blocking collectives, on_device(): lax.psum((grad_gain1, grad_shift1, grad_in_bias, grad_out_bias, grad_gain...  41.1 us
    all_to_all x1, blocking collectives, on_device(): lax.all_to_all(mixed.astype(jnp.bfloat16), 'seq', split_axis=1, concat_ax...  40.9 us
    dot_general x4, matrix products, forward_real(): jnp.einsum('kn,cnq->ckq', cos_p[:, :half_rows], blocked, precision=HIGH)  38.2 us
  transfers between devices with their start and end apart: 16, of which 7 were waited for; matrix products, arithmetic and copies ran while one was open for 19% of the time, Pallas kernels for 0%

profile of v1, /device:TPU:0, one launch (start us, length us, event | category | flops | bytes accessed | tf_op | source)
XLA Modules:
  0.0 1580.8 jit_solution(4491395435882854591)
XLA Ops:
  50.7 9.5 fusion.127
  75.5 14.0 collective-permute-done.4
  101.3 9.3 fusion.131
  110.6 9.5 fusion.133
  120.2 12.3 fusion.24
  152.4 9.2 fusion.64
  161.6 9.6 fusion.87
  171.2 9.1 fusion.90
  180.3 9.4 fusion.81
  189.7 14.2 multiply_subtract_fusion
  221.4 18.1 %fusion.44 = f32[128,64,64]{0,2,1:T(8,128)S(1)} fusion(f32[128,64]{0,1:T(8,128)S(1)} %get-tuple-element.111, f32[128,64]{0,1:T(8,128)S(1)} %get-tuple-element.112, f32[128,128,64]{1,2,0:T(8,128)S(1)} %fusion.184, f32[128,128,64]{1,2,0:T(8,128)S(1)} %fusion.202, f32[128,128,64]{1,2,0:T(8,128)S(1)} %fusion.182, f32[128,128,64]{1,2,0:T(8,128)S(1)} %fusion.200, ...), kind=kOutput, calls=%fused_computation.88 | convolution fusion | flops 810549248 | bytes 19005440 | tf_op jit(solution)/shard_map/jvp(nk,ckq->cnq)/dot_general | solution.py:93
  239.5 21.2 %multiply_bitcast_fusion = f32[128,64,64]{0,1,2:T(8,128)S(1)} fusion(f32[128,64,64]{0,2,1:T(8,128)S(1)} %fusion.44, f32[128,64]{0,1:T(8,128)S(1)} %get-tuple-element.111, f32[128,64]{0,1:T(8,128)S(1)} %get-tuple-element.112, f32[128,128,64]{1,2,0:T(8,128)S(1)} %fusion.184, f32[128,128,64]{1,2,0:T(8,128)S(1)} %fusion.202, f32[128,128,64]{1,2,0:T(8,128)S(1)} %fusion.182, ...), kind=kOutput, calls=%fused_computation.183 | convolution fusion | flops 811597824 | bytes 21102592 | tf_op jit(solution)/shard_map/jvp(nk,ckq->cnq)/dot_general | solution.py:93
  262.6 40.9 %all_to_all.47 = bf16[128,8,512]{0,2,1:T(8,128)(2,1)} all-to-all(bf16[128,8,512]{0,2,1:T(8,128)(2,1)S(1)} %fusion.118), channel_id=1, replica_groups=mesh['dp'=4,'seq'=8] {'seq'}, dimensions={1} | all-to-all | bytes 2097152 | tf_op jit(solution)/shard_map/all_to_all | solution.py:230
  308.8 10.8 fusion.353
  319.6 16.2 %convert_reduce_fusion = (f32[4096]{0:T(1024)}, bf16[512,4096]{1,0:T(8,128)(2,1)}) fusion(f32[512,4096]{1,0:T(8,128)} %fusion.353, f32[4096]{0:T(1024)S(1)} %copy-done.75, bf16[4096,1024]{1,0:T(8,128)(2,1)} %param.42, bf16[1,512,1024]{2,1,0:T(8,128)(2,1)S(1)} %copy-done.28), kind=kOutput, calls=%fused_computation.9 | convolution fusion | flops 4343197696 | bytes 22052864 | tf_op jit(solution)/shard_map/td,fd->tf/dot_general | solution.py:248
  357.6 36.0 %all-to-all-done.1 = bf16[8,128,512]{1,2,0:T(8,128)(2,1)} async-done(((bf16[8,128,512]{1,2,0:T(8,128)(2,1)}), bf16[8,128,512]{1,2,0:T(8,128)(2,1)}, u32[]{:S(2)}, u32[]{:S(2)}) %all-to-all-start.1) | async-done | bytes 1048608 | tf_op jit(solution)/shard_map/all_to_all | solution.py:267
  418.6 9.6 fusion.38
  428.2 9.3 fusion.96
  437.5 17.6 %multiply_add_fusion.2 = (f32[128,128,64]{1,2,0:T(8,128)S(1)}, f32[128,128,64]{1,2,0:T(8,128)}, f32[128,128,64]{1,2,0:T(8,128)}, f32[128,128,64]{1,2,0:T(8,128)}) fusion(f32[128,128,64]{1,2,0:T(8,128)} %get-tuple-element.103, f32[128,128,64]{1,2,0:T(8,128)} %fusion.81, f32[128,128,64]{1,2,0:T(8,128)} %fusion.96, f32[128,128,64]{1,2,0:T(8,128)} %fusion.87, ...), kind=kOutput, calls=%fused_computation.83 | convolution fusion | flops 820043776 | bytes 46137344 | tf_op jit(solution)/shard_map/transpose(jvp(ckm,nm->ckn))/dot_general | solution.py:88
  490.8 12.2 fusion.14
  503.0 9.3 fusion.32
  541.1 20.0 %copy.241 = bf16[3,128,4096]{1,0,2:T(4,128)(2,1)S(1)} copy(bf16[3,128,4096]{1,2,0:T(8,128)(2,1)S(1)} %fusion.9) | data formatting | bytes 6291456 | tf_op jit(solution)/shard_map/convert_element_type | solution.py:281
  561.1 93.1 %all_to_all.48 = bf16[3,128,4096]{1,0,2:T(4,128)(2,1)S(1)} all-to-all(bf16[3,128,4096]{1,0,2:T(4,128)(2,1)S(1)} %copy.241), channel_id=1, replica_groups=mesh['dp'=4,'seq'=8] {'seq'}, dimensions={2} | all-to-all | bytes 6291456 | tf_op jit(solution)/shard_map/all_to_all | solution.py:280
  670.1 13.3 fusion.352
  683.5 15.8 fusion.144
  700.0 176.7 %reduce-scatter.9.cloned.1.call-done = f32[128,3072]{1,0:T(8,128)} async-done(((f32[1024,3072]{1,0:T(8,128)}), f32[128,3072]{1,0:T(8,128)}) %reduce-scatter.9.cloned.1.call-update) | async-done | bytes 1572880 | tf_op jit(solution)/shard_map/reduce_scatter | solution.py:137
  876.8 286.0 %reduce-scatter.17.cloned.1.call-done = f32[128,4096]{1,0:T(8,128)} async-done(((f32[1024,4096]{1,0:T(8,128)}), f32[128,4096]{1,0:T(8,128)}) %reduce-scatter.17.cloned.1.call-update) | async-done | bytes 2097168 | tf_op jit(solution)/shard_map/reduce_scatter | solution.py:139
  1163.1 13.0 fusion.142
  1192.9 255.3 %reduce-scatter.21.cloned.1.call-done = f32[512,1024]{1,0:T(8,128)} async-done(((f32[4096,1024]{1,0:T(8,128)}), f32[512,1024]{1,0:T(8,128)}) %reduce-scatter.21.cloned.1.call-update) | async-done | bytes 2097168 | tf_op jit(solution)/shard_map/reduce_scatter | solution.py:140
  1460.9 12.7 all-reduce.11
  1492.0 41.1 %all-reduce.10 = (f32[1024]{0:T(1024)}, f32[1024]{0:T(1024)}, f32[3072]{0:T(1024)}, f32[33,64]{1,0:T(8,128)}, f32[64]{0:T(128)}, /*index=5*/f32[64]{0:T(128)}, f...) all-reduce(f32[1024]{0:T(1024)S(1)} %get-tuple-element.29, ...), channel_id=1, replica_groups=mesh['dp'=4,'seq'=8] {'dp','seq'}, use_global_device_ids=true, to_apply=%region_9.10 | all-reduce | flops 15552 | bytes 124416 | tf_op jit(solution)/shard_map/psum | solution.py:290
  1539.2 34.4 %reduce-scatter.23.cloned.1.call-done = f32[512,256]{1,0:T(8,128)} async-done(((f32[512,1024]{1,0:T(8,128)}), f32[512,256]{1,0:T(8,128)}) %reduce-scatter.23.cloned.1.call-update) | async-done | bytes 524304 | tf_op jit(solution)/shard_map/reduce_scatter | solution.py:146
  (301 shorter events, 296.2 us)
Async XLA Ops:
  7.2 298.6 %copy-start = (bf16[1024,1024]{1,0:T(8,128)(2,1)S(1)}, bf16[1024,1024]{1,0:T(8,128)(2,1)}, u32[]{:S(2)}) copy-start(bf16[1024,1024]{1,0:T(8,128)(2,1)} %param.36) | copy-start | bytes 6291460
  29.1 35.5 %collective-permute-start = (bf16[3,128,512]{1,2,0:T(8,128)(2,1)}, bf16[3,128,512]{1,2,0:T(8,128)(2,1)}, u32[]{:S(2)}, u32[]{:S(2)}) collective-permute-start(bf16[3,128,512]{1,2,0:T(8,128)(2,1)} %get-tuple-element.90), channel_id=1, source_target_pairs={{0,1},{1,0},{2,3},{3,2},{4,5},{5,4},{6,7},{7,6},{8,9},{9,8},{10,11... | collective-permute-start | bytes 1179656 | tf_op jit(solution)/shard_map/ppermute | solution.py:196
  32.1 38.0 %collective-permute-start.1 = (bf16[3,128,512]{1,2,0:T(8,128)(2,1)}, bf16[3,128,512]{1,2,0:T(8,128)(2,1)}, u32[]{:S(2)}, u32[]{:S(2)}) collective-permute-start(bf16[3,128,512]{1,2,0:T(8,128)(2,1)} %get-tuple-element.89), channel_id=1, source_target_pairs={{0,2},{1,3},{2,0},{3,1},{4,6},{5,7},{6,4},{7,5},{8,10},{9,11},{10,... | collective-permute-start | bytes 1179656 | tf_op jit(solution)/shard_map/ppermute | solution.py:196
  33.6 38.3 %collective-permute-start.2 = (bf16[3,128,512]{1,2,0:T(8,128)(2,1)}, bf16[3,128,512]{1,2,0:T(8,128)(2,1)}, u32[]{:S(2)}, u32[]{:S(2)}) collective-permute-start(bf16[3,128,512]{1,2,0:T(8,128)(2,1)} %get-tuple-element.88), channel_id=1, source_target_pairs={{0,3},{1,2},{2,1},{3,0},{4,7},{5,6},{6,5},{7,4},{8,11},{9,10},{10,... | collective-permute-start | bytes 1179656 | tf_op jit(solution)/shard_map/ppermute | solution.py:196
  33.6 40.1 %collective-permute-start.3 = (bf16[3,128,512]{1,2,0:T(8,128)(2,1)}, bf16[3,128,512]{1,2,0:T(8,128)(2,1)}, u32[]{:S(2)}, u32[]{:S(2)}) collective-permute-start(bf16[3,128,512]{1,2,0:T(8,128)(2,1)} %get-tuple-element.87), channel_id=1, source_target_pairs={{0,4},{1,5},{2,6},{3,7},{4,0},{5,1},{6,2},{7,3},{8,12},{9,13},{10,... | collective-permute-start | bytes 1179656 | tf_op jit(solution)/shard_map/ppermute | solution.py:196
  36.6 52.9 %collective-permute-start.4 = (bf16[3,128,512]{1,2,0:T(8,128)(2,1)}, bf16[3,128,512]{1,2,0:T(8,128)(2,1)}, u32[]{:S(2)}, u32[]{:S(2)}) collective-permute-start(bf16[3,128,512]{1,2,0:T(8,128)(2,1)} %get-tuple-element.86), channel_id=1, source_target_pairs={{0,5},{1,4},{2,7},{3,6},{4,1},{5,0},{6,3},{7,2},{8,13},{9,12},{10,... | collective-permute-start | bytes 1179656 | tf_op jit(solution)/shard_map/ppermute | solution.py:196
  60.2 35.1 %copy-start.53 = (f32[3,128]{1,0:T(4,128)}, f32[3,128]{1,0:T(4,128)S(1)}, u32[]{:S(2)}) copy-start(f32[3,128]{1,0:T(4,128)S(1)} %get-tuple-element.101) | copy-start | bytes 4612
  60.2 35.1 %copy-start.55 = (f32[3,128]{1,0:T(4,128)}, f32[3,128]{1,0:T(4,128)S(1)}, u32[]{:S(2)}) copy-start(f32[3,128]{1,0:T(4,128)S(1)} %get-tuple-element.100) | copy-start | bytes 4612
  60.3 35.1 %copy-start.57 = (f32[3,128]{1,0:T(4,128)}, f32[3,128]{1,0:T(4,128)S(1)}, u32[]{:S(2)}) copy-start(f32[3,128]{1,0:T(4,128)S(1)} %get-tuple-element.102) | copy-start | bytes 4612
  64.6 26.8 %collective-permute-start.5 = (bf16[3,128,512]{1,2,0:T(8,128)(2,1)}, bf16[3,128,512]{1,2,0:T(8,128)(2,1)S(1)}, u32[]{:S(2)}, u32[]{:S(2)}) collective-permute-start(bf16[3,128,512]{1,2,0:T(8,128)(2,1)} %get-tuple-element.85), channel_id=1, source_target_pairs={{0,6},{1,7},{2,4},{3,5},{4,2},{5,3},{6,0},{7,1},{8,14},{9,15},{10,... | collective-permute-start | bytes 1179656 | tf_op jit(solution)/shard_map/ppermute | solution.py:196
  70.1 22.1 %collective-permute-start.6 = (bf16[3,128,512]{1,2,0:T(8,128)(2,1)}, bf16[3,128,512]{1,2,0:T(8,128)(2,1)S(1)}, u32[]{:S(2)}, u32[]{:S(2)}) collective-permute-start(bf16[3,128,512]{1,2,0:T(8,128)(2,1)} %get-tuple-element.84), channel_id=1, source_target_pairs={{0,7},{1,6},{2,5},{3,4},{4,3},{5,2},{6,1},{7,0},{8,15},{9,14},{10,... | collective-permute-start | bytes 1179656 | tf_op jit(solution)/shard_map/ppermute | solution.py:196
  101.3 160.7 %copy-start.2 = (f32[1,128,4096]{1,2,0:T(8,128)}, f32[1,128,4096]{1,2,0:T(8,128)S(1)}, u32[]{:S(2)}) copy-start(f32[1,128,4096]{1,2,0:T(8,128)S(1)} %get-tuple-element.80) | copy-start | bytes 6291460
  261.9 41.6 %copy-start.18 = (f32[128,64,64]{0,2,1:T(8,128)}, f32[128,64,64]{0,2,1:T(8,128)S(1)}, u32[]{:S(2)}) copy-start(f32[128,64,64]{0,2,1:T(8,128)S(1)} %copy.222) | copy-start | bytes 6291460
  262.3 43.5 %copy-start.43 = (f32[1024]{0:T(1024)S(1)}, f32[1024]{0:T(1024)}, u32[]{:S(2)}) copy-start(f32[1024]{0:T(1024)} %param.37) | copy-start | bytes 12292
  308.4 35.5 %copy-start.15 = (f32[512,1024]{1,0:T(8,128)}, f32[512,1024]{1,0:T(8,128)S(1)}, u32[]{:S(2)}) copy-start(f32[512,1024]{1,0:T(8,128)S(1)} %get-tuple-element.105) | copy-start | bytes 6291460
  308.8 27.1 %slice-start.4 = ((s8[8388608]{0:T(1024)(128)(4,1)}), s8[4194304]{0:T(1024)(128)(4,1)S(1)}, s32[]{:S(2)}) async-start(s8[8388608]{0:T(1024)(128)(4,1)} %bitcast.405), calls=%async_computation.23 | async-start | bytes 8388608
  348.5 45.1 %all-to-all-start.1 = ((bf16[8,128,512]{1,2,0:T(8,128)(2,1)}), bf16[8,128,512]{1,2,0:T(8,128)(2,1)}, u32[]{:S(2)}, u32[]{:S(2)}) async-start(bf16[8,128,512]{1,2,0:T(8,128)(2,1)} %bitcast.377), calls=%async_computation.1 | async-start | bytes 2097152 | tf_op jit(solution)/shard_map/all_to_all | solution.py:267
  352.7 346.7 %reduce-scatter.13.cloned.1.call-start = ((), (), s32[]{:S(2)}) async-start(), calls=%async_computation.13 | async-start | bytes 4718592 | tf_op jit(solution)/shard_map/reduce_scatter | solution.py:138
  357.4 37.6 %copy-start.17 = (f32[1,128,4096]{1,2,0:T(8,128)S(1)}, f32[1,128,4096]{1,2,0:T(8,128)}, u32[]{:S(2)}) copy-start(f32[1,128,4096]{1,2,0:T(8,128)} %get-tuple-element.81) | copy-start | bytes 6291460
  357.4 519.3 %reduce-scatter.9.cloned.1.call-start = ((), (), s32[]{:S(2)}) async-start(), calls=%async_computation.11 | async-start | bytes 14155776 | tf_op jit(solution)/shard_map/reduce_scatter | solution.py:137
  670.1 492.8 %reduce-scatter.17.cloned.1.call-start = ((), (), s32[]{:S(2)}) async-start(), calls=%async_computation.15 | async-start | bytes 18874368 | tf_op jit(solution)/shard_map/reduce_scatter | solution.py:139
  683.5 764.7 %reduce-scatter.21.cloned.1.call-start = ((), (), s32[]{:S(2)}) async-start(), calls=%async_computation.17 | async-start | bytes 18874368 | tf_op jit(solution)/shard_map/reduce_scatter | solution.py:140
  699.3 463.7 %copy-start.79 = (f32[1024]{0:T(1024)S(1)}, f32[1024]{0:T(1024)}, u32[]{:S(2)}) copy-start(f32[1024]{0:T(1024)} %param.43) | copy-start | bytes 12292
  699.4 833.7 %reduce-scatter.15.cloned.1.call-start = ((), (), s32[]{:S(2)}) async-start(), calls=%async_computation.14 | async-start | bytes 655360 | tf_op jit(solution)/shard_map/reduce_scatter | solution.py:144
  699.9 833.1 %reduce-scatter.11.cloned.1.call-start = ((), (), s32[]{:S(2)}) async-start(), calls=%async_computation.12 | async-start | bytes 1966080 | tf_op jit(solution)/shard_map/reduce_scatter | solution.py:143
  876.7 662.5 %reduce-scatter.19.cloned.1.call-start = ((), (), s32[]{:S(2)}) async-start(), calls=%async_computation.16 | async-start | bytes 2621440 | tf_op jit(solution)/shard_map/reduce_scatter | solution.py:145
  1162.9 410.8 %reduce-scatter.23.cloned.1.call-start = ((), (), s32[]{:S(2)}) async-start(), calls=%async_computation.18 | async-start | bytes 2621440 | tf_op jit(solution)/shard_map/reduce_scatter | solution.py:146
  1190.3 257.9 %copy-start.40 = (f32[4096]{0:T(1024)S(1)}, f32[4096]{0:T(1024)}, u32[]{:S(2)}) copy-start(f32[4096]{0:T(1024)} %copy-done.39) | copy-start | bytes 49156
  1190.3 257.9 %copy-start.71 = (f32[128]{0:T(128)S(1)}, f32[128]{0:T(128)}, u32[]{:S(2)}) copy-start(f32[128]{0:T(128)} %copy-done.70) | copy-start | bytes 1540
  1192.9 258.7 %copy-start.65 = (f32[64]{0:T(128)S(1)}, f32[64]{0:T(128)}, u32[]{:S(2)}) copy-start(f32[64]{0:T(128)} %param.32) | copy-start | bytes 772
  1458.4 22.6 %copy-start.33 = (f32[16,4096]{1,0:T(8,128)S(1)}, f32[16,4096]{1,0:T(8,128)}, u32[]{:S(2)}) copy-start(f32[16,4096]{1,0:T(8,128)} %copy-done.32) | copy-start | bytes 786436
  1489.2 84.5 %copy-start.1 = (bf16[1024,1024]{1,0:T(8,128)(2,1)S(1)}, bf16[1024,1024]{1,0:T(8,128)(2,1)}, u32[]{:S(2)}) copy-start(bf16[1024,1024]{1,0:T(8,128)(2,1)} %param.36) | copy-start | bytes 6291460
  (71 other events, 512.2 us)
Sparse Core Ops, SparseCore 0:
  357.5 97.4 reduce-scatter.12
  670.2 206.4 reduce-scatter.8
  881.0 281.8 reduce-scatter.16
  1166.5 281.6 reduce-scatter.20
  1451.2 21.1 reduce-scatter.14
  1475.4 28.4 reduce-scatter.10
  1507.1 32.0 reduce-scatter.18
  1542.3 31.2 reduce-scatter.22
